TPU v7x, 32 devices: a whole 2x2x4 slice. The times are simulated.
32 devices in a mesh: pipe: 4 (over x, core), row: 4 (over z), col: 2 (over y).
Axes of the slice: x: 2, y: 2, z: 4, core: 2. Of those that a mesh axis runs over, the one named last changes fastest.
Arguments:
- handoff: bfloat16 [4, 256, 12288], P('pipe', 'col', 'row'), may hold values from -1200 to 1200
- norm_gain: float32 [4, 12288], P('pipe', 'row'), may hold values from 0.1 to 1.9
- norm_shift: float32 [4, 12288], P('pipe', 'row'), may hold values from -3 to 3
- up_weight: bfloat16 [4, 12288, 24576], P('pipe', 'row', 'col'), may hold values from -0.0546875 to 0.0546875
- up_bias: float32 [4, 24576], P('pipe', 'col'), may hold values from -3 to 3
Outputs:
- hidden: bfloat16 [4, 256, 24576], P('pipe', 'row', 'col')
All inputs are finite; a program needn't handle non-finite values.
Results may differ from a plain program's by a relative error of at most 0.018.
Values may be sent and summed in bfloat16 or wider, within the bound.
A program may use at most 128 MiB of HBM per device.

v0:
```python
import jax
import jax.numpy as jnp
from jax import lax
from jax.sharding import PartitionSpec as P

epsilon = 1e-05


def passed_along(value, axis, steps):
    count = lax.axis_size(axis)
    pairs = [(source, (source + steps) % count) for source in range(count)]
    return lax.ppermute(value, axis, pairs)


def normalize(values, row_total, squares, feature_gain, feature_shift, feature_count):
    center = (row_total / feature_count)[:, None]
    spread_sq = (squares / feature_count)[:, None] - center * center
    inverse = lax.rsqrt(spread_sq + epsilon)
    return ((values - center) * inverse * feature_gain + feature_shift).astype(jnp.bfloat16)


def local(handoff, norm_gain, norm_shift, up_weight, up_bias):
    arrived = passed_along(handoff[0], "pipe", 1)
    feature_gain = norm_gain[0]
    feature_shift = norm_shift[0]
    weight_block = up_weight[0]
    bias_block = up_bias[0]
    feature_count = arrived.shape[1] * lax.axis_size("row")
    values = arrived.astype(jnp.float32)
    row_total, squares = lax.psum(
        (jnp.sum(values, axis=1), jnp.sum(values * values, axis=1)), "row"
    )
    own_normed = normalize(values, row_total, squares, feature_gain, feature_shift, feature_count)
    normed = lax.all_gather(own_normed, "col", axis=0, tiled=True)
    summed = lax.psum_scatter(
        jnp.dot(normed, weight_block, preferred_element_type=jnp.float32).astype(jnp.bfloat16),
        "row",
        scatter_dimension=0,
        tiled=True,
    ).astype(jnp.float32)
    preact = summed + bias_block
    return jax.nn.gelu(preact, approximate=True).astype(jnp.bfloat16)[None]


def solution(mesh):
    in_specs = (
        P("pipe", "col", "row"),
        P("pipe", "row"),
        P("pipe", "row"),
        P("pipe", "row", "col"),
        P("pipe", "col"),
    )
    out_specs = P("pipe", "row", "col")
    return jax.shard_map(local, mesh=mesh, in_specs=in_specs, out_specs=out_specs, check_vma=False)
```

profile of v0, /device:TPU:0, one launch (start us, length us, event | category | flops | bytes accessed | tf_op | source)
XLA Modules:
  0.0 212.2 jit_solution(13344893527006407649)
XLA Ops:
  6.5 0.0 all-gather.2.cloned.1.call-start
  6.5 0.5 collective-permute-start
  7.0 11.8 %collective-permute-done = bf16[128,3072]{1,0:T(8,128)(2,1)S(1)} collective-permute-done((bf16[128,3072]{1,0:T(8,128)(2,1)}, bf16[128,3072]{1,0:T(8,128)(2,1)S(1)}, u32[]{:S(2)}, u32[]{:S(2)}) %collective-permute-start) | collective-permute-done | bytes 786464 | tf_op jit(solution)/shard_map/ppermute | solution.py:12
  18.8 0.3 convert_reduce_fusion
  19.1 12.8 %all-reduce = (f32[128]{0:T(128)S(1)}, f32[128]{0:T(128)S(1)}) all-reduce(f32[128]{0:T(128)S(1)} %get-tuple-element.6, f32[128]{0:T(128)S(1)} %get-tuple-element.5), channel_id=1, replica_groups=mesh['pipe'=4,'row'=4,'col'=2] {'row'}, use_global_device_ids=true, to_apply=%region_3.0 | all-reduce | flops 256 | bytes 2048 | tf_op jit(solution)/shard_map/psum | solution.py:30
  31.9 2.0 fusion.16
  33.9 0.0 all-gather.2.cloned.1.call-update
  33.9 0.0 reduce-scatter.2.cloned.1.call-start
  34.0 25.5 %all-gather.2.cloned.1.call-done = bf16[256,3072]{1,0:T(8,128)(2,1)} async-done(((bf16[128,3072]{1,0:T(8,128)(2,1)}), bf16[256,3072]{1,0:T(8,128)(2,1)}) %all-gather.2.cloned.1.call-update) | async-done | bytes 1572880 | tf_op jit(solution)/shard_map/all_gather | solution.py:34
  59.5 31.2 %fusion.2 = bf16[256,12288]{1,0:T(8,128)(2,1)} fusion(bf16[256,3072]{1,0:T(8,128)(2,1)} %all-gather.2.cloned.1.call-done, bf16[1,3072,12288]{2,1,0:T(8,128)(2,1)} %param.8), kind=kOutput, calls=%fused_computation.2 | convolution fusion | flops 19330498560 | bytes 83361792 | tf_op jit(solution)/shard_map/dot_general | solution.py:36
  90.6 0.0 copy-start
  90.6 0.0 reduce-scatter.2.cloned.1.call-update
  90.7 110.9 %reduce-scatter.2.cloned.1.call-done = bf16[64,12288]{1,0:T(8,128)(2,1)} async-done(((bf16[256,12288]{1,0:T(8,128)(2,1)}), bf16[64,12288]{1,0:T(8,128)(2,1)}) %reduce-scatter.2.cloned.1.call-update) | async-done | bytes 1572880 | tf_op jit(solution)/shard_map/reduce_scatter | solution.py:35
  201.6 0.0 copy-done
  201.6 3.7 %fusion.18 = bf16[1,64,12288]{2,1,0:T(8,128)(2,1)} fusion(bf16[64,12288]{1,0:T(8,128)(2,1)} %reduce-scatter.2.cloned.1.call-done, f32[12288]{0:T(1024)S(1)} %bitcast.12), kind=kLoop, calls=%fused_computation.20 | loop fusion | flops 8650752 | bytes 3194880 | tf_op jit(solution)/shard_map/broadcast_in_dim | solution.py:42
  (1 shorter events, 0.0 us)
Async XLA Ops:
  6.5 52.9 %all-gather.2.cloned.1.call-start = ((), (), s32[]{:S(2)}) async-start(), calls=%async_computation.1 | async-start | bytes 2359296 | tf_op jit(solution)/shard_map/all_gather | solution.py:34
  6.5 12.3 %collective-permute-start = (bf16[128,3072]{1,0:T(8,128)(2,1)}, bf16[128,3072]{1,0:T(8,128)(2,1)S(1)}, u32[]{:S(2)}, u32[]{:S(2)}) collective-permute-start(bf16[128,3072]{1,0:T(8,128)(2,1)} %bitcast.15), channel_id=1, source_target_pairs={{0,8},{8,16},{16,24},{24,0},{1,9},{9,17},{17,25},{25,1},{2,10},{10... | collective-permute-start | bytes 2359304 | tf_op jit(solution)/shard_map/ppermute | solution.py:12
  33.9 167.7 %reduce-scatter.2.cloned.1.call-start = ((), (), s32[]{:S(2)}) async-start(), calls=%async_computation.2 | async-start | bytes 7864320 | tf_op jit(solution)/shard_map/reduce_scatter | solution.py:35
  90.6 111.0 %copy-start = (f32[1,12288]{1,0:T(1,128)S(1)}, f32[1,12288]{1,0:T(1,128)}, u32[]{:S(2)}) copy-start(f32[1,12288]{1,0:T(1,128)} %param.9) | copy-start | bytes 147460
Sparse Core Ops, SparseCore 0:
  34.0 25.3 all-gather.1
  90.8 110.7 reduce-scatter.1
where the time goes:
time: 212 us
  waiting for transfers between devices  148 us (70%)
  matrix products  31.2 us (15%)
  between operations  13.4 us (6%)
  blocking collectives  12.8 us (6%)
  other arithmetic  6.01 us (3%)
    reduce_scatter x1, waiting for transfers between devices, local(): lax.psum_scatter(jnp.dot(normed, weight_block, preferred_element_type=jnp...  111 us
    dot_general x1, matrix products, local(): jnp.dot(normed, weight_block, preferred_element_type=jnp.float32)  31.2 us
    all_gather x1, waiting for transfers between devices, local(): normed = lax.all_gather(own_normed, 'col', axis=0, tiled=True)  25.5 us
    psum x1, blocking collectives, local(): lax.psum((jnp.sum(values, axis=1), jnp.sum(values * values, axis=1)), 'row')  12.8 us
    ppermute x1, waiting for transfers between devices, passed_along(): return lax.ppermute(value, axis, pairs)  11.8 us
  transfers between devices with their start and end apart: 3, of which 3 were waited for; matrix products, arithmetic and copies ran while one was open for 0% of the time, Pallas kernels for 0%

commit v1 on v0

--- a/solution.py
+++ b/solution.py
@@ -4,6 +4,28 @@
 from jax.sharding import PartitionSpec as P
 
 epsilon = 1e-05
+
+
+def in_order(blocks, dim):
+    blocks = jnp.moveaxis(blocks, 0, dim)
+    shape = blocks.shape
+    return blocks.reshape(*shape[:dim], shape[dim] * shape[dim + 1], *shape[dim + 2 :])
+
+
+def doubled(shard, axis):
+    size = lax.axis_size(axis)
+    tiles = shard[None]
+    for level in range(size.bit_length() - 1):
+        apart = 1 << level
+        other = lax.ppermute(tiles, axis, [(i, i ^ apart) for i in range(size)])
+        both = jnp.stack([tiles, other])
+        upper = lax.axis_index(axis) >> level & 1
+        tiles = jnp.where(upper == 0, both, both[::-1]).reshape(-1, *shard.shape)
+    return tiles
+
+
+def doubled_up(x, axis, dim):
+    return in_order(doubled(x, axis), dim)
 
 
 def passed_along(value, axis, steps):
@@ -31,7 +53,7 @@
         (jnp.sum(values, axis=1), jnp.sum(values * values, axis=1)), "row"
     )
     own_normed = normalize(values, row_total, squares, feature_gain, feature_shift, feature_count)
-    normed = lax.all_gather(own_normed, "col", axis=0, tiled=True)
+    normed = doubled_up(own_normed, "col", 0)
     summed = lax.psum_scatter(
         jnp.dot(normed, weight_block, preferred_element_type=jnp.float32).astype(jnp.bfloat16),
         "row",

time: 212 us -> 202 us (0.953)
  waiting for transfers between devices: 148 us -> 135 us
    all_gather x1 -> x0, waiting for transfers between devices: 25.5 us -> none  [local(): normed = lax.all_gather(own_normed, 'col', axis=0, tiled=True)]
    ppermute x0 -> x1, waiting for transfers between devices: none -> 15.1 us  [doubled(): other = lax.ppermute(tiles, axis, [(i, i ^ apart) for i in range(size)])]
    reduce_scatter x1, waiting for transfers between devices: 111 us -> 108 us  [local(): lax.psum_scatter(jnp.dot(normed, weight_block, preferred_element_type=jnp...]
where the time goes in v1:
time: 202 us; the launch traced here: 201 us
  waiting for transfers between devices  135 us (67%)
  matrix products  32.1 us (16%)
  between operations  13.4 us (7%)
  blocking collectives  12.8 us (6%)
  other arithmetic  5.68 us (3%)
  starting transfers between devices  2.08 us (1%)
    reduce_scatter x1, waiting for transfers between devices, local(): lax.psum_scatter(jnp.dot(normed, weight_block, preferred_element_type=jnp...  108 us
    dot_general x1, matrix products, local(): jnp.dot(normed, weight_block, preferred_element_type=jnp.float32)  32.1 us
    ppermute x1, waiting for transfers between devices, doubled(): other = lax.ppermute(tiles, axis, [(i, i ^ apart) for i in range(size)])  15.1 us
    psum x1, blocking collectives, local(): lax.psum((jnp.sum(values, axis=1), jnp.sum(values * values, axis=1)), 'row')  12.8 us
    ppermute x1, waiting for transfers between devices, passed_along(): return lax.ppermute(value, axis, pairs)  11.8 us
  transfers between devices with their start and end apart: 3, of which 3 were waited for; matrix products, arithmetic and copies ran while one was open for 0% of the time, Pallas kernels for 0%

profile of v1, /device:TPU:0, one launch (start us, length us, event | category | flops | bytes accessed | tf_op | source)
XLA Modules:
  0.0 201.2 jit_solution(7908120483561139065)
XLA Ops:
  6.5 0.0 reduce-scatter.2.cloned.1.call-start
  6.5 0.5 collective-permute-start
  7.0 11.8 %collective-permute-done = bf16[128,3072]{1,0:T(8,128)(2,1)S(1)} collective-permute-done((bf16[128,3072]{1,0:T(8,128)(2,1)}, bf16[128,3072]{1,0:T(8,128)(2,1)S(1)}, u32[]{:S(2)}, u32[]{:S(2)}) %collective-permute-start) | collective-permute-done | bytes 786464 | tf_op jit(solution)/shard_map/ppermute | solution.py:34
  18.8 0.3 convert_reduce_fusion
  19.1 12.8 %all-reduce = (f32[128]{0:T(128)S(1)}, f32[128]{0:T(128)S(1)}) all-reduce(f32[128]{0:T(128)S(1)} %get-tuple-element.6, f32[128]{0:T(128)S(1)} %get-tuple-element.5), channel_id=1, replica_groups=mesh['pipe'=4,'row'=4,'col'=2] {'row'}, use_global_device_ids=true, to_apply=%region_3.0 | all-reduce | flops 256 | bytes 2048 | tf_op jit(solution)/shard_map/psum | solution.py:52
  31.9 1.2 fusion.20
  33.1 1.6 collective-permute-start.1
  34.7 15.1 %collective-permute-done.1 = bf16[1,128,3072]{2,1,0:T(8,128)(2,1)S(1)} collective-permute-done((bf16[1,128,3072]{2,1,0:T(8,128)(2,1)S(1)}, bf16[1,128,3072]{2,1,0:T(8,128)(2,1)S(1)}, u32[]{:S(2)}, u32[]{:S(2)}) %collective-permute-start.1) | collective-permute-done | bytes 786464 | tf_op jit(solution)/shard_map/ppermute | solution.py:20
  49.8 0.1 pad_maximum_fusion
  50.0 0.3 reverse_select_fusion
  50.3 32.1 %fusion.2 = bf16[256,12288]{1,0:T(8,128)(2,1)} fusion(bf16[256,3072]{1,0:T(8,128)(2,1)S(1)} %bitcast.18, bf16[1,3072,12288]{2,1,0:T(8,128)(2,1)} %param.8), kind=kOutput, calls=%fused_computation.2 | convolution fusion | flops 19330498560 | bytes 83361792 | tf_op jit(solution)/shard_map/dot_general | solution.py:58
  82.4 0.0 copy-start
  82.4 0.0 reduce-scatter.2.cloned.1.call-update
  82.4 108.2 %reduce-scatter.2.cloned.1.call-done = bf16[64,12288]{1,0:T(8,128)(2,1)} async-done(((bf16[256,12288]{1,0:T(8,128)(2,1)}), bf16[64,12288]{1,0:T(8,128)(2,1)}) %reduce-scatter.2.cloned.1.call-update) | async-done | bytes 1572880 | tf_op jit(solution)/shard_map/reduce_scatter | solution.py:57
  190.6 0.0 copy-done
  190.6 3.7 %fusion.18 = bf16[1,64,12288]{2,1,0:T(8,128)(2,1)} fusion(bf16[64,12288]{1,0:T(8,128)(2,1)} %reduce-scatter.2.cloned.1.call-done, f32[12288]{0:T(1024)S(1)} %bitcast.20), kind=kLoop, calls=%fused_computation.21 | loop fusion | flops 8650752 | bytes 3194880 | tf_op jit(solution)/shard_map/broadcast_in_dim | solution.py:64
  (1 shorter events, 0.0 us)
Async XLA Ops:
  6.5 184.1 %reduce-scatter.2.cloned.1.call-start = ((), (), s32[]{:S(2)}) async-start(), calls=%async_computation.1 | async-start | bytes 7864320 | tf_op jit(solution)/shard_map/reduce_scatter | solution.py:57
  6.5 12.3 %collective-permute-start = (bf16[128,3072]{1,0:T(8,128)(2,1)}, bf16[128,3072]{1,0:T(8,128)(2,1)S(1)}, u32[]{:S(2)}, u32[]{:S(2)}) collective-permute-start(bf16[128,3072]{1,0:T(8,128)(2,1)} %bitcast.23), channel_id=1, source_target_pairs={{0,8},{8,16},{16,24},{24,0},{1,9},{9,17},{17,25},{25,1},{2,10},{10... | collective-permute-start | bytes 2359304 | tf_op jit(solution)/shard_map/ppermute | solution.py:34
  33.1 16.7 %collective-permute-start.1 = (bf16[1,128,3072]{2,1,0:T(8,128)(2,1)S(1)}, bf16[1,128,3072]{2,1,0:T(8,128)(2,1)S(1)}, u32[]{:S(2)}, u32[]{:S(2)}) collective-permute-start(bf16[1,128,3072]{2,1,0:T(8,128)(2,1)S(1)} %get-tuple-element.10), channel_id=1, source_target_pairs={{0,1},{1,0},{2,3},{3,2},{4,5},{5,4},{6,7},{7,6},{8,9},{9,8},{10,11... | collective-permute-start | bytes 2359304 | tf_op jit(solution)/shard_map/ppermute | solution.py:20
  82.4 108.2 %copy-start = (f32[1,12288]{1,0:T(1,128)S(1)}, f32[1,12288]{1,0:T(1,128)}, u32[]{:S(2)}) copy-start(f32[1,12288]{1,0:T(1,128)} %param.9) | copy-start | bytes 147460
Sparse Core Ops, SparseCore 0:
  82.5 108.0 reduce-scatter.1
